TPU v7x, 256 devices: a whole 4x4x8 slice. The times are simulated.
256 devices in a mesh: tok: 16 (over y, x), col: 16 (over z, core).
Axes of the slice: x: 4, y: 4, z: 8, core: 2. Of those that a mesh axis runs over, the one named last changes fastest.
Arguments:
- activations: bfloat16 [32768, 8192], P('tok', 'col'), may hold values from -60 to 60, as said below
- weight: bfloat16 [8192, 8192], P('tok', 'col'), may hold values from -6 to 6
- keep_mask: int32 [8192, 8192], P('tok', 'col'), may hold values from 0 to 1
Outputs:
- new_weight: bfloat16 [8192, 8192], P('tok', 'col')
Inputs may be any that keep to these rules, and one draw needn't show every extreme that they name: activations of calibration tokens.
All inputs are finite; a program needn't handle non-finite values.
Results may differ from a plain program's by a relative error of at most 0.00115.
Values may be sent and summed in bfloat16 or wider, within the bound.
A program may use at most 64 MiB of HBM per device.

v0:
```python
import jax
import jax.numpy as jnp
from jax import lax
from jax.sharding import PartitionSpec as P

B = 1024
ITERS = 4


def per_device(activations, weight, keep_mask):
    highest = lax.Precision.HIGHEST
    n_col = lax.axis_size("col")
    n_tok = lax.axis_size("tok")
    tok_rows = activations.shape[0]
    panel_width = B // n_col
    total_count = tok_rows * n_tok
    partial_panel = lax.dot_general(
        activations,
        lax.all_gather(activations[:, :panel_width], "col", axis=1, tiled=True),
        (((0,), (0,)), ((), ())),
        preferred_element_type=jnp.float32,
    )
    hessian_panel = lax.psum(partial_panel, "tok") / total_count
    block_part = hessian_panel[:panel_width]
    diagonal_block = lax.all_gather(block_part, "col", axis=0, tiled=True)
    identity = jnp.eye(B, dtype=jnp.float32)
    damping = 0.01 * jnp.mean(jnp.diagonal(diagonal_block))
    damped = diagonal_block + damping * identity
    frobenius = jnp.sqrt(jnp.sum(damped * damped))
    col_index = lax.axis_index("col")
    row_ids = col_index * panel_width + lax.iota(jnp.int32, panel_width)
    iterate = (row_ids[:, None] == lax.iota(jnp.int32, B)[None, :]).astype(jnp.float32) / frobenius
    for sweep in range(ITERS):
        if sweep == 0:
            whole = identity / frobenius
        else:
            whole = lax.all_gather(iterate.astype(jnp.bfloat16), "col", axis=0, tiled=True).astype(
                iterate.dtype
            )
        product = jnp.dot(iterate, damped, precision=highest)
        iterate = 2.0 * iterate - jnp.dot(product, whole, precision=highest)
    inverse = lax.all_gather(iterate, "col", axis=0, tiled=True)
    pruned = jnp.where(
        keep_mask[:, :panel_width] == 0, weight[:, :panel_width], jnp.zeros((), jnp.bfloat16)
    )
    pruned_panel = lax.all_gather(pruned, "col", axis=1, tiled=True).astype(jnp.float32)
    factor_rows = jnp.dot(pruned_panel, inverse, precision=highest)
    correction = lax.dot_general(
        factor_rows, hessian_panel, (((1,), (1,)), ((), ())), precision=highest
    )
    kept = keep_mask.astype(jnp.float32)
    return (kept * (weight.astype(jnp.float32) - correction)).astype(jnp.bfloat16)


def solution(mesh):
    return jax.shard_map(
        per_device,
        mesh=mesh,
        in_specs=(P("tok", "col"), P("tok", "col"), P("tok", "col")),
        out_specs=P("tok", "col"),
        check_vma=False,
    )
```

profile of v0, /device:TPU:1, one launch (start us, length us, event | category | flops | bytes accessed | tf_op | source)
XLA Modules:
  0.0 456.3 jit_solution(11155648659330884020)
XLA Ops:
  6.5 0.0 all-gather.10.cloned.1.call-start
  6.5 1.1 slice.14
  7.6 0.9 copy.9
  8.5 0.0 all-gather.10.cloned.1.call-update
  8.5 0.0 all-reduce.2.cloned.1.call-start
  8.6 47.0 %all-gather.10.cloned.1.call-done = bf16[2048,1024]{0,1:T(8,128)(2,1)} async-done(((bf16[2048,64]{0,1:T(8,128)(2,1)}), bf16[2048,1024]{0,1:T(8,128)(2,1)}) %all-gather.10.cloned.1.call-update) | async-done | bytes 4194320 | tf_op jit(solution)/shard_map/all_gather | solution.py:19
  55.5 6.6 %fusion.25 = f32[512,1024]{1,0:T(8,128)} fusion(bf16[2048,512]{1,0:T(8,128)(2,1)} %param.3, bf16[2048,1024]{0,1:T(8,128)(2,1)} %all-gather.10.cloned.1.call-done), kind=kOutput, calls=%fused_computation.37 | convolution fusion | flops 2147483648 | bytes 8388608 | tf_op jit(solution)/shard_map/dot_general | solution.py:17
  62.1 0.0 all-reduce.2.cloned.1.call-update
  62.2 0.0 all-gather.12.cloned.1.call-start
  62.2 97.5 %all-reduce.2.cloned.1.call-done = f32[512,1024]{1,0:T(8,128)} async-done(((f32[512,1024]{1,0:T(8,128)}), f32[512,1024]{1,0:T(8,128)}) %all-reduce.2.cloned.1.call-update) | async-done | bytes 2097168 | tf_op jit(solution)/shard_map/psum | solution.py:23
  159.7 1.8 broadcast_multiply_fusion
  161.5 0.7 slice.18
  162.2 0.0 all-gather.12.cloned.1.call-update
  162.3 0.0 all-gather.14.cloned.1.call-start
  162.3 43.1 %all-gather.12.cloned.1.call-done = f32[1024,1024]{1,0:T(8,128)} async-done(((f32[64,1024]{1,0:T(8,128)}), f32[1024,1024]{1,0:T(8,128)}) %all-gather.12.cloned.1.call-update) | async-done | bytes 4194320 | tf_op jit(solution)/shard_map/all_gather | solution.py:25
  205.5 17.2 %gather_fusion = f32[1024]{0:T(1024)S(1)} fusion(f32[1024,1024]{1,0:T(8,128)} %all-gather.12.cloned.1.call-done, s32[1024]{0:T(1024)S(1)} %bitcast.16), kind=kCustom, calls=%fused_computation | custom fusion | bytes 16384 | tf_op jit(solution)/shard_map/jit(diagonal)/cond/branch_0_fun/gather | solution.py:27
  222.7 0.6 reduce_sum.18
  223.9 3.9 multiply_reduce_fusion
  228.5 4.9 %fusion.9 = f32[64,1024]{1,0:T(8,128)S(1)} fusion(f32[1024,1024]{1,0:T(8,128)} %all-gather.12.cloned.1.call-done, f32[]{:T(128)S(6)} %mul_shard_map.3, f32[]{:T(128)S(6)} %sqrt.3, s32[64]{0:T(128)S(1)} %iota_add_fusion), kind=kOutput, calls=%fused_computation.14 | convolution fusion | flops 808583168 | bytes 4456712 | tf_op jit(solution)/shard_map/dot_general | solution.py:40
  233.4 1.9 fusion.22
  235.3 0.0 all-gather.14.cloned.1.call-update
  235.3 0.0 all-gather.16.cloned.1.call-start
  235.4 4.9 %fusion.8 = f32[64,1024]{1,0:T(8,128)S(1)} fusion(f32[64,1024]{1,0:T(8,128)S(1)} %get-tuple-element.6, f32[1024,1024]{1,0:T(8,128)} %all-gather.12.cloned.1.call-done, f32[]{:T(128)S(6)} %mul_shard_map.3), kind=kOutput, calls=%fused_computation.13 | convolution fusion | flops 808452096 | bytes 4718596 | tf_op jit(solution)/shard_map/dot_general | solution.py:40
  240.3 33.5 %all-gather.14.cloned.1.call-done = bf16[1024,1024]{1,0:T(8,128)(2,1)} async-done(((bf16[64,1024]{1,0:T(8,128)(2,1)}), bf16[1024,1024]{1,0:T(8,128)(2,1)}) %all-gather.14.cloned.1.call-update) | async-done | bytes 2097168 | tf_op jit(solution)/shard_map/all_gather | solution.py:37
  273.8 3.5 fusion.23
  277.3 0.0 all-gather.16.cloned.1.call-update
  277.3 0.2 all-gather.18.cloned.1.call-start
  277.5 0.0 slice-start
  277.5 0.0 slice-start.1
  277.5 4.9 %fusion.7 = f32[64,1024]{1,0:T(8,128)S(1)} fusion(f32[64,1024]{1,0:T(8,128)S(1)} %get-tuple-element.8, f32[1024,1024]{1,0:T(8,128)} %all-gather.12.cloned.1.call-done, f32[]{:T(128)S(6)} %mul_shard_map.3), kind=kOutput, calls=%fused_computation.12 | convolution fusion | flops 808452096 | bytes 4718596 | tf_op jit(solution)/shard_map/dot_general | solution.py:40
  282.5 33.0 %all-gather.16.cloned.1.call-done = bf16[1024,1024]{1,0:T(8,128)(2,1)} async-done(((bf16[64,1024]{1,0:T(8,128)(2,1)}), bf16[1024,1024]{1,0:T(8,128)(2,1)}) %all-gather.16.cloned.1.call-update) | async-done | bytes 2097168 | tf_op jit(solution)/shard_map/all_gather | solution.py:37
  315.5 3.5 fusion.24
  318.9 0.0 all-gather.18.cloned.1.call-update
  319.0 0.0 all-gather.8.cloned.1.call-start
  319.0 0.0 slice-done
  319.0 0.1 copy.7
  319.1 0.0 slice-done.1
  319.1 0.1 copy.8
  319.3 0.6 compare_select_fusion
  319.9 0.0 all-gather.8.cloned.1.call-update
  319.9 0.0 all-gather.20.cloned.1.call-start
  320.0 4.9 %fusion.6 = f32[64,1024]{1,0:T(8,128)S(1)} fusion(f32[64,1024]{1,0:T(8,128)S(1)} %get-tuple-element.10, f32[1024,1024]{1,0:T(8,128)} %all-gather.12.cloned.1.call-done, f32[]{:T(128)S(6)} %mul_shard_map.3), kind=kOutput, calls=%fused_computation.11 | convolution fusion | flops 808452096 | bytes 4718596 | tf_op jit(solution)/shard_map/dot_general | solution.py:40
  324.9 32.3 %all-gather.18.cloned.1.call-done = bf16[1024,1024]{1,0:T(8,128)(2,1)} async-done(((bf16[64,1024]{1,0:T(8,128)(2,1)}), bf16[1024,1024]{1,0:T(8,128)(2,1)}) %all-gather.18.cloned.1.call-update) | async-done | bytes 2097168 | tf_op jit(solution)/shard_map/all_gather | solution.py:37
  357.2 3.5 convolution_subtract_fusion.1
  360.7 0.0 copy-start
  360.7 0.0 copy-start.1
  360.7 0.0 all-gather.20.cloned.1.call-update
  360.7 35.4 %all-gather.8.cloned.1.call-done = bf16[512,1024]{0,1:T(8,128)(2,1)} async-done(((bf16[512,64]{0,1:T(8,128)(2,1)}), bf16[512,1024]{0,1:T(8,128)(2,1)}) %all-gather.8.cloned.1.call-update) | async-done | bytes 1048592 | tf_op jit(solution)/shard_map/all_gather | solution.py:46
  396.1 42.8 %all-gather.20.cloned.1.call-done = f32[1024,1024]{1,0:T(8,128)} async-done(((f32[64,1024]{1,0:T(8,128)}), f32[1024,1024]{1,0:T(8,128)}) %all-gather.20.cloned.1.call-update) | async-done | bytes 4194320 | tf_op jit(solution)/shard_map/all_gather | solution.py:42
  438.9 0.0 copy-start.2
  438.9 6.1 %fusion.26 = f32[512,1024]{1,0:T(8,128)S(1)} fusion(bf16[512,1024]{0,1:T(8,128)(2,1)} %all-gather.8.cloned.1.call-done, f32[1024,1024]{1,0:T(8,128)} %all-gather.20.cloned.1.call-done), kind=kOutput, calls=%fused_computation.38 | convolution fusion | flops 6442450944 | bytes 7340032 | tf_op jit(solution)/shard_map/dot_general | solution.py:47
  445.0 0.0 copy-done
  445.0 0.0 copy-done.1
  445.0 0.0 copy-done.2
  445.0 4.5 fusion.5
  (2 shorter events, 0.0 us)
Async XLA Ops:
  6.5 49.0 %all-gather.10.cloned.1.call-start = ((), (), s32[]{:S(2)}) async-start(), calls=%async_computation.1 | async-start | bytes 4456448 | tf_op jit(solution)/shard_map/all_gather | solution.py:19
  8.5 151.2 %all-reduce.2.cloned.1.call-start = ((), (), s32[]{:S(2)}) async-start(), calls=%async_computation.2 | async-start | bytes 4194304 | tf_op jit(solution)/shard_map/psum | solution.py:23
  62.2 143.3 %all-gather.12.cloned.1.call-start = ((), (), s32[]{:S(2)}) async-start(), calls=%async_computation.3 | async-start | bytes 4456448 | tf_op jit(solution)/shard_map/all_gather | solution.py:25
  162.3 111.5 %all-gather.14.cloned.1.call-start = ((), (), s32[]{:S(2)}) async-start(), calls=%async_computation.4 | async-start | bytes 2228224 | tf_op jit(solution)/shard_map/all_gather | solution.py:37
  235.3 80.1 %all-gather.16.cloned.1.call-start = ((), (), s32[]{:S(2)}) async-start(), calls=%async_computation.5 | async-start | bytes 2228224 | tf_op jit(solution)/shard_map/all_gather | solution.py:37
  277.3 79.9 %all-gather.18.cloned.1.call-start = ((), (), s32[]{:S(2)}) async-start(), calls=%async_computation.6 | async-start | bytes 2228224 | tf_op jit(solution)/shard_map/all_gather | solution.py:37
  277.5 41.5 %slice-start = ((s32[512,512]{1,0:T(8,128)}), s32[512,64]{1,0:T(8,128)S(1)}, s32[]{:S(2)}) async-start(s32[512,512]{1,0:T(8,128)} %param.5), calls=%async_computation.8 | async-start | bytes 524288 | tf_op jit(solution)/shard_map/slice | solution.py:44
  277.5 41.6 %slice-start.1 = ((bf16[512,512]{1,0:T(8,128)(2,1)}), bf16[512,64]{1,0:T(8,128)(2,1)S(1)}, s32[]{:S(2)}) async-start(bf16[512,512]{1,0:T(8,128)(2,1)} %param.4), calls=%async_computation.9 | async-start | bytes 262144 | tf_op jit(solution)/shard_map/slice | solution.py:44
  319.0 77.2 %all-gather.8.cloned.1.call-start = ((), (), s32[]{:S(2)}) async-start(), calls=%async_computation | async-start | bytes 1114112 | tf_op jit(solution)/shard_map/all_gather | solution.py:46
  319.9 119.0 %all-gather.20.cloned.1.call-start = ((), (), s32[]{:S(2)}) async-start(), calls=%async_computation.7 | async-start | bytes 4456448 | tf_op jit(solution)/shard_map/all_gather | solution.py:42
  360.7 84.3 %copy-start = (f32[512,1024]{1,0:T(8,128)S(1)}, f32[512,1024]{1,0:T(8,128)}, u32[]{:S(2)}) copy-start(f32[512,1024]{1,0:T(8,128)} %all-reduce.2.cloned.1.call-done) | copy-start | bytes 6291460
  360.7 84.3 %copy-start.1 = (s32[512,512]{1,0:T(8,128)S(1)}, s32[512,512]{1,0:T(8,128)}, u32[]{:S(2)}) copy-start(s32[512,512]{1,0:T(8,128)} %param.5) | copy-start | bytes 3145732
  438.9 6.1 %copy-start.2 = (bf16[512,512]{1,0:T(8,128)(2,1)S(1)}, bf16[512,512]{1,0:T(8,128)(2,1)}, u32[]{:S(2)}) copy-start(bf16[512,512]{1,0:T(8,128)(2,1)} %param.4) | copy-start | bytes 1572868
Sparse Core Ops, SparseCore 0:
  9.2 46.3 all-gather.9
  62.3 97.4 all-reduce.1
  162.4 43.0 all-gather.11
  235.5 38.2 all-gather.13
  277.4 38.0 all-gather.15
  319.1 38.0 all-gather.17
  359.1 36.9 all-gather.7
  398.1 40.7 all-gather.19
where the time goes:
time: 457 us; the launch traced here: 456 us
  waiting for transfers between devices  365 us (80%)
  matrix products  49.1 us (11%)
  local copies, waits for them, and re-layouts  20.1 us (4%)
  between operations  15 us (3%)
  other arithmetic  6.89 us (2%)
    all_gather x3, waiting for transfers between devices, per_device(): lax.all_gather(iterate.astype(jnp.bfloat16), 'col', axis=0, tiled=True)  98.8 us
    psum x1, waiting for transfers between devices, per_device(): hessian_panel = lax.psum(partial_panel, 'tok') / total_count  97.5 us
    all_gather x1, waiting for transfers between devices, per_device(): lax.all_gather(activations[:, :panel_width], 'col', axis=1, tiled=True)  47 us
    all_gather x1, waiting for transfers between devices, per_device(): diagonal_block = lax.all_gather(block_part, 'col', axis=0, tiled=True)  43.1 us
    all_gather x1, waiting for transfers between devices, per_device(): inverse = lax.all_gather(iterate, 'col', axis=0, tiled=True)  42.8 us
    all_gather x1, waiting for transfers between devices, per_device(): lax.all_gather(pruned, 'col', axis=1, tiled=True).astype(jnp.float32)  35.4 us
    dot_general x4, matrix products, per_device(): product = jnp.dot(iterate, damped, precision=highest)  19.6 us
    gather x1, local copies, waits for them, and re-layouts, per_device(): damping = 0.01 * jnp.mean(jnp.diagonal(diagonal_block))  17.2 us
  transfers between devices with their start and end apart: 8, of which 8 were waited for; matrix products, arithmetic and copies ran while one was open for 4% of the time, Pallas kernels for 0%

commit v1 on v0

--- a/solution.py
+++ b/solution.py
@@ -20,7 +20,7 @@
         (((0,), (0,)), ((), ())),
         preferred_element_type=jnp.float32,
     )
-    hessian_panel = lax.psum(partial_panel, "tok") / total_count
+    hessian_panel = jnp.sum(lax.all_gather(partial_panel, "tok"), axis=0) / total_count
     block_part = hessian_panel[:panel_width]
     diagonal_block = lax.all_gather(block_part, "col", axis=0, tiled=True)
     identity = jnp.eye(B, dtype=jnp.float32)

time: 457 us -> 569 us (1.25)
  waiting for transfers between devices: 365 us -> 466 us
  other arithmetic: 6.89 us -> 17.4 us
    all_gather x0 -> x1, waiting for transfers between devices: none -> 200 us  [per_device(): lax.all_gather(partial_panel, 'tok')]
    psum x1 -> x0, waiting for transfers between devices: 97.5 us -> none  [per_device(): hessian_panel = lax.psum(partial_panel, 'tok') / total_count]
    reduce_sum x0 -> x1, other arithmetic: none -> 12.1 us  [per_device(): jnp.sum(lax.all_gather(partial_panel, 'tok'), axis=0) / total_count]
  transfers between devices with their start and end apart: 8 -> 8, of which waited for: 8 -> 8; matrix products, arithmetic and copies ran while one was open for 4% -> 3% of each run, Pallas kernels for 0% -> 0%
where the time goes in v1:
time: 569 us; the launch traced here: 568 us
  waiting for transfers between devices  466 us (82%)
  matrix products  49 us (9%)
  local copies, waits for them, and re-layouts  19.6 us (3%)
  other arithmetic  17.4 us (3%)
  between operations  15 us (3%)
    all_gather x1, waiting for transfers between devices, per_device(): lax.all_gather(partial_panel, 'tok')  200 us
    all_gather x3, waiting for transfers between devices, per_device(): lax.all_gather(iterate.astype(jnp.bfloat16), 'col', axis=0, tiled=True)  98.8 us
    all_gather x1, waiting for transfers between devices, per_device(): lax.all_gather(activations[:, :panel_width], 'col', axis=1, tiled=True)  47 us
    all_gather x1, waiting for transfers between devices, per_device(): inverse = lax.all_gather(iterate, 'col', axis=0, tiled=True)  42.7 us
    all_gather x1, waiting for transfers between devices, per_device(): diagonal_block = lax.all_gather(block_part, 'col', axis=0, tiled=True)  42.4 us
    all_gather x1, waiting for transfers between devices, per_device(): lax.all_gather(pruned, 'col', axis=1, tiled=True).astype(jnp.float32)  35.2 us
    dot_general x4, matrix products, per_device(): product = jnp.dot(iterate, damped, precision=highest)  19.6 us
    gather x1, local copies, waits for them, and re-layouts, per_device(): damping = 0.01 * jnp.mean(jnp.diagonal(diagonal_block))  16.7 us
  transfers between devices with their start and end apart: 8, of which 8 were waited for; matrix products, arithmetic and copies ran while one was open for 3% of the time, Pallas kernels for 0%

profile of v1, /device:TPU:1, one launch (start us, length us, event | category | flops | bytes accessed | tf_op | source)
XLA Modules:
  0.0 567.9 jit_solution(3921698860223621381)
XLA Ops:
  6.5 0.0 all-gather.12.cloned.1.call-start
  6.5 1.1 slice.14
  7.6 0.9 copy.9
  8.5 0.0 all-gather.12.cloned.1.call-update
  8.5 0.0 all-gather.24.cloned.1.call-start
  8.6 47.0 %all-gather.12.cloned.1.call-done = bf16[2048,1024]{0,1:T(8,128)(2,1)} async-done(((bf16[2048,64]{0,1:T(8,128)(2,1)}), bf16[2048,1024]{0,1:T(8,128)(2,1)}) %all-gather.12.cloned.1.call-update) | async-done | bytes 4194320 | tf_op jit(solution)/shard_map/all_gather | solution.py:19
  55.5 6.5 %fusion.25 = f32[512,1024]{1,0:T(8,128)} fusion(bf16[2048,512]{1,0:T(8,128)(2,1)} %param.3, bf16[2048,1024]{0,1:T(8,128)(2,1)} %all-gather.12.cloned.1.call-done), kind=kOutput, calls=%fused_computation.37 | convolution fusion | flops 2147483648 | bytes 8388608 | tf_op jit(solution)/shard_map/dot_general | solution.py:17
  62.1 0.0 all-gather.24.cloned.1.call-update
  62.1 0.0 all-gather.14.cloned.1.call-start
  62.1 200.3 %all-gather.24.cloned.1.call-done = f32[8192,1024]{1,0:T(8,128)} async-done(((f32[512,1024]{1,0:T(8,128)}), f32[8192,1024]{1,0:T(8,128)}) %all-gather.24.cloned.1.call-update) | async-done | bytes 33554448 | tf_op jit(solution)/shard_map/all_gather | solution.py:23
  262.5 12.1 %reduce_sum.27 = f32[512,1024]{1,0:T(8,128)S(1)} reduce(f32[16,512,1024]{2,1,0:T(8,128)} %bitcast.18, f32[]{:T(128)} %constant.28.clone.1), dimensions={0}, to_apply=%region_0.0 | reduce | flops 7864320 | bytes 35651588 | tf_op jit(solution)/shard_map/reduce_sum | solution.py:23
  274.6 0.2 broadcast_multiply_fusion
  274.8 0.7 slice.18
  275.5 0.0 all-gather.14.cloned.1.call-update
  275.5 0.0 all-gather.16.cloned.1.call-start
  275.6 42.4 %all-gather.14.cloned.1.call-done = f32[1024,1024]{1,0:T(8,128)} async-done(((f32[64,1024]{1,0:T(8,128)}), f32[1024,1024]{1,0:T(8,128)}) %all-gather.14.cloned.1.call-update) | async-done | bytes 4194320 | tf_op jit(solution)/shard_map/all_gather | solution.py:25
  318.0 16.7 %gather_fusion = f32[1024]{0:T(1024)S(1)} fusion(f32[1024,1024]{1,0:T(8,128)} %all-gather.14.cloned.1.call-done, s32[1024]{0:T(1024)S(1)} %bitcast.17), kind=kCustom, calls=%fused_computation | custom fusion | bytes 16384 | tf_op jit(solution)/shard_map/jit(diagonal)/cond/branch_0_fun/gather | solution.py:27
  334.7 0.6 reduce_sum.28
  335.9 3.9 multiply_reduce_fusion
  340.5 4.9 fusion.9
  345.4 1.9 fusion.22
  347.3 0.0 all-gather.16.cloned.1.call-update
  347.3 0.0 all-gather.18.cloned.1.call-start
  347.4 4.9 fusion.8
  352.3 33.5 %all-gather.16.cloned.1.call-done = bf16[1024,1024]{1,0:T(8,128)(2,1)} async-done(((bf16[64,1024]{1,0:T(8,128)(2,1)}), bf16[1024,1024]{1,0:T(8,128)(2,1)}) %all-gather.16.cloned.1.call-update) | async-done | bytes 2097168 | tf_op jit(solution)/shard_map/all_gather | solution.py:37
  385.8 3.5 fusion.23
  389.3 0.0 all-gather.18.cloned.1.call-update
  389.3 0.2 all-gather.20.cloned.1.call-start
  389.5 0.0 slice-start
  389.5 0.0 slice-start.1
  389.5 4.9 fusion.7
  394.5 33.0 %all-gather.18.cloned.1.call-done = bf16[1024,1024]{1,0:T(8,128)(2,1)} async-done(((bf16[64,1024]{1,0:T(8,128)(2,1)}), bf16[1024,1024]{1,0:T(8,128)(2,1)}) %all-gather.18.cloned.1.call-update) | async-done | bytes 2097168 | tf_op jit(solution)/shard_map/all_gather | solution.py:37
  427.5 3.5 fusion.24
  430.9 0.0 all-gather.20.cloned.1.call-update
  431.0 0.0 all-gather.10.cloned.1.call-start
  431.0 0.0 slice-done
  431.0 0.1 copy.7
  431.1 0.0 slice-done.1
  431.1 0.1 copy.8
  431.2 0.6 compare_select_fusion
  431.9 0.0 all-gather.10.cloned.1.call-update
  431.9 0.0 all-gather.22.cloned.1.call-start
  432.0 4.9 fusion.6
  436.9 32.3 %all-gather.20.cloned.1.call-done = bf16[1024,1024]{1,0:T(8,128)(2,1)} async-done(((bf16[64,1024]{1,0:T(8,128)(2,1)}), bf16[1024,1024]{1,0:T(8,128)(2,1)}) %all-gather.20.cloned.1.call-update) | async-done | bytes 2097168 | tf_op jit(solution)/shard_map/all_gather | solution.py:37
  469.1 3.5 convolution_subtract_fusion.1
  472.7 0.0 copy-start
  472.7 0.0 all-gather.22.cloned.1.call-update
  472.7 35.2 %all-gather.10.cloned.1.call-done = bf16[512,1024]{0,1:T(8,128)(2,1)} async-done(((bf16[512,64]{0,1:T(8,128)(2,1)}), bf16[512,1024]{0,1:T(8,128)(2,1)}) %all-gather.10.cloned.1.call-update) | async-done | bytes 1048592 | tf_op jit(solution)/shard_map/all_gather | solution.py:46
  507.9 42.7 %all-gather.22.cloned.1.call-done = f32[1024,1024]{1,0:T(8,128)} async-done(((f32[64,1024]{1,0:T(8,128)}), f32[1024,1024]{1,0:T(8,128)}) %all-gather.22.cloned.1.call-update) | async-done | bytes 4194320 | tf_op jit(solution)/shard_map/all_gather | solution.py:42
  550.5 0.0 copy-start.1
  550.5 6.1 %fusion.26 = f32[512,1024]{1,0:T(8,128)S(1)} fusion(bf16[512,1024]{0,1:T(8,128)(2,1)} %all-gather.10.cloned.1.call-done, f32[1024,1024]{1,0:T(8,128)} %all-gather.22.cloned.1.call-done), kind=kOutput, calls=%fused_computation.38 | convolution fusion | flops 6442450944 | bytes 7340032 | tf_op jit(solution)/shard_map/dot_general | solution.py:47
  556.6 0.0 copy-done
  556.6 0.0 copy-done.1
  556.6 4.5 fusion.5
  (2 shorter events, 0.0 us)
Async XLA Ops:
  6.5 49.0 %all-gather.12.cloned.1.call-start = ((), (), s32[]{:S(2)}) async-start(), calls=%async_computation.1 | async-start | bytes 4456448 | tf_op jit(solution)/shard_map/all_gather | solution.py:19
  8.5 253.9 %all-gather.24.cloned.1.call-start = ((), (), s32[]{:S(2)}) async-start(), calls=%async_computation.7 | async-start | bytes 35651584 | tf_op jit(solution)/shard_map/all_gather | solution.py:23
  62.1 255.9 %all-gather.14.cloned.1.call-start = ((), (), s32[]{:S(2)}) async-start(), calls=%async_computation.2 | async-start | bytes 4456448 | tf_op jit(solution)/shard_map/all_gather | solution.py:25
  275.5 110.3 %all-gather.16.cloned.1.call-start = ((), (), s32[]{:S(2)}) async-start(), calls=%async_computation.3 | async-start | bytes 2228224 | tf_op jit(solution)/shard_map/all_gather | solution.py:37
  347.3 80.1 %all-gather.18.cloned.1.call-start = ((), (), s32[]{:S(2)}) async-start(), calls=%async_computation.4 | async-start | bytes 2228224 | tf_op jit(solution)/shard_map/all_gather | solution.py:37
  389.3 79.9 %all-gather.20.cloned.1.call-start = ((), (), s32[]{:S(2)}) async-start(), calls=%async_computation.5 | async-start | bytes 2228224 | tf_op jit(solution)/shard_map/all_gather | solution.py:37
  389.5 41.5 %slice-start = ((s32[512,512]{1,0:T(8,128)}), s32[512,64]{1,0:T(8,128)S(1)}, s32[]{:S(2)}) async-start(s32[512,512]{1,0:T(8,128)} %param.5), calls=%async_computation.8 | async-start | bytes 524288 | tf_op jit(solution)/shard_map/slice | solution.py:44
  389.5 41.6 %slice-start.1 = ((bf16[512,512]{1,0:T(8,128)(2,1)}), bf16[512,64]{1,0:T(8,128)(2,1)S(1)}, s32[]{:S(2)}) async-start(bf16[512,512]{1,0:T(8,128)(2,1)} %param.4), calls=%async_computation.9 | async-start | bytes 262144 | tf_op jit(solution)/shard_map/slice | solution.py:44
  431.0 76.9 %all-gather.10.cloned.1.call-start = ((), (), s32[]{:S(2)}) async-start(), calls=%async_computation | async-start | bytes 1114112 | tf_op jit(solution)/shard_map/all_gather | solution.py:46
  431.9 118.6 %all-gather.22.cloned.1.call-start = ((), (), s32[]{:S(2)}) async-start(), calls=%async_computation.6 | async-start | bytes 4456448 | tf_op jit(solution)/shard_map/all_gather | solution.py:42
  472.7 84.0 %copy-start = (s32[512,512]{1,0:T(8,128)S(1)}, s32[512,512]{1,0:T(8,128)}, u32[]{:S(2)}) copy-start(s32[512,512]{1,0:T(8,128)} %param.5) | copy-start | bytes 3145732
  550.5 6.1 %copy-start.1 = (bf16[512,512]{1,0:T(8,128)(2,1)S(1)}, bf16[512,512]{1,0:T(8,128)(2,1)}, u32[]{:S(2)}) copy-start(bf16[512,512]{1,0:T(8,128)(2,1)} %param.4) | copy-start | bytes 1572868
Sparse Core Ops, SparseCore 0:
  9.2 46.3 all-gather.11
  62.2 200.2 all-gather.23
  275.6 42.2 all-gather.13
  347.5 38.2 all-gather.15
  389.4 38.0 all-gather.17
  431.1 38.0 all-gather.19
  471.0 36.8 all-gather.9
  509.7 40.7 all-gather.21
